TPU v7x, 256 devices: a whole 4x4x8 slice. The times are simulated.
256 devices in a mesh: prow: 32 (over z_hi, y, x), pcol: 8 (over z_lo, core).
Axes of the slice: x: 4, y: 4, z: 8 (z_hi: 2, z_lo: 4; z = z_hi * 4 + z_lo), core: 2. Of those that a mesh axis runs over, the one named last changes fastest.
Arguments:
- eigen_rows: float32 [1024, 229376], P(('pcol', 'prow')), may hold values from -6 to 6
- reflectors: float32 [229376, 512], P('prow', 'pcol'), may hold values from -0.375 to 0.375
- tfactors: float32 [2, 256, 256], replicated, may hold values from -0.01171875 to 0.01171875
Outputs:
- back_rows: float32 [1024, 229376], P('pcol', 'prow')
All inputs are finite; a program needn't handle non-finite values.
Results may differ from a plain program's by a relative error of at most 0.000084.
Values sent between devices are 32-bit elements; how exact they have to be, the bound alone decides.
No kernel may reach another device: no remote copies, remote signals or barrier semaphores. Data moves between devices by JAX's collectives and lax.ppermute only.
A program may use at most 128 MiB of HBM per device.

v0:
```python
import jax
import jax.numpy as jnp
from jax import lax
from jax.sharding import PartitionSpec as P


def upper_part(square):
    width = square.shape[0]
    rows = lax.broadcasted_iota(jnp.int32, (width, width), 0)
    cols = lax.broadcasted_iota(jnp.int32, (width, width), 1)
    return jnp.where(cols >= rows, square, jnp.zeros_like(square))


def matmul(left, right):
    return jnp.dot(left, right, precision=lax.Precision.HIGHEST, preferred_element_type=jnp.float32)


def apply_both(matrix, vectors, tfactors, summer):
    width = tfactors.shape[1]
    first_tri = upper_part(tfactors[0])
    second_tri = upper_part(tfactors[1])
    for panel_index in (1, 0):
        panel_vectors = vectors[:, panel_index * width : (panel_index + 1) * width]
        triangle = second_tri if panel_index == 1 else first_tri
        projected = summer(matmul(matrix, panel_vectors))
        matrix = matrix - matmul(matmul(projected, triangle.T), panel_vectors.T)
    return matrix


def body(eigen_rows, reflectors, tfactors):
    grid_rows = lax.all_to_all(eigen_rows, "prow", split_axis=1, concat_axis=0, tiled=True)
    grid_vectors = lax.all_gather(reflectors, "pcol", axis=1, tiled=True)

    def summer_grid(values):
        return lax.psum(values, "prow")

    return apply_both(grid_rows, grid_vectors, tfactors, summer_grid)


def solution(mesh):
    return jax.shard_map(
        body,
        mesh=mesh,
        in_specs=(P(("pcol", "prow"), None), P("prow", "pcol"), P()),
        out_specs=P("pcol", "prow"),
        check_vma=False,
    )
```

profile of v0, /device:TPU:32, one launch (start us, length us, event | category | flops | bytes accessed | tf_op | source)
XLA Modules:
  0.0 1083.6 jit_solution(4444081856075703498)
XLA Ops:
  6.5 0.0 all-gather.2.cloned.1.call-start
  6.5 0.7 all-gather.2.cloned.1.call-update
  7.3 0.0 all-reduce.3.cloned.1.call-start
  7.3 139.8 %all_to_all.19 = f32[4,32,7168]{2,0,1:T(4,128)} all-to-all(f32[4,32,7168]{2,0,1:T(4,128)} %bitcast.15), channel_id=1, replica_groups=mesh['prow'=32,'pcol'=8] {'prow'}, dimensions={1} | all-to-all | bytes 7340032 | tf_op jit(solution)/shard_map/all_to_all | solution.py:31
  147.1 5.3 all_to_all.17
  152.3 0.0 copy-start.2
  152.3 86.0 %all-gather.2.cloned.1.call-done = f32[7168,512]{0,1:T(8,128)} async-done(((f32[7168,64]{0,1:T(8,128)}), f32[7168,512]{0,1:T(8,128)}) %all-gather.2.cloned.1.call-update) | async-done | bytes 14680080 | tf_op jit(solution)/shard_map/all_gather | solution.py:32
  238.4 12.3 %fusion.4 = f32[128,256]{1,0:T(8,128)} fusion(f32[128,7168]{1,0:T(8,128)} %all_to_all.17, f32[7168,512]{0,1:T(8,128)} %all-gather.2.cloned.1.call-done), kind=kOutput, calls=%fused_computation.6 | convolution fusion | flops 2818572288 | bytes 11141120 | tf_op jit(solution)/shard_map/dot_general | solution.py:15
  250.6 0.0 all-reduce.3.cloned.1.call-update
  250.6 0.2 all-reduce.5.cloned.1.call-start
  250.9 398.6 %all-reduce.3.cloned.1.call-done = f32[128,256]{1,0:T(8,128)} async-done(((f32[128,256]{1,0:T(8,128)}), f32[128,256]{1,0:T(8,128)}) %all-reduce.3.cloned.1.call-update) | async-done | bytes 131088 | tf_op jit(solution)/shard_map/psum | solution.py:35
  649.4 0.0 copy-done.2
  649.4 1.3 fusion.7
  650.7 0.0 copy-start
  650.8 9.2 convolution_subtract_fusion.1
  660.0 0.0 copy-start.1
  660.0 1.8 copy-done.1
  661.8 0.0 copy-done
  661.8 8.1 fusion.1
  669.9 0.0 all-reduce.5.cloned.1.call-update
  669.9 395.6 %all-reduce.5.cloned.1.call-done = f32[128,256]{1,0:T(8,128)} async-done(((f32[128,256]{1,0:T(8,128)}), f32[128,256]{1,0:T(8,128)}) %all-reduce.5.cloned.1.call-update) | async-done | bytes 131088 | tf_op jit(solution)/shard_map/psum | solution.py:35
  1065.4 1.3 fusion.6
  1066.8 10.3 convolution_subtract_fusion
Async XLA Ops:
  6.5 231.8 %all-gather.2.cloned.1.call-start = ((), (), s32[]{:S(2)}) async-start(), calls=%async_computation.1 | async-start | bytes 16515072 | tf_op jit(solution)/shard_map/all_gather | solution.py:32
  7.3 642.2 %all-reduce.3.cloned.1.call-start = ((), (), s32[]{:S(2)}) async-start(), calls=%async_computation.2 | async-start | bytes 262144 | tf_op jit(solution)/shard_map/psum | solution.py:35
  152.3 497.1 %copy-start.2 = (f32[2,256,256]{2,1,0:T(8,128)S(1)}, f32[2,256,256]{2,1,0:T(8,128)}, u32[]{:S(2)}) copy-start(f32[2,256,256]{2,1,0:T(8,128)} %param.5) | copy-start | bytes 1572868
  250.6 814.8 %all-reduce.5.cloned.1.call-start = ((), (), s32[]{:S(2)}) async-start(), calls=%async_computation.3 | async-start | bytes 262144 | tf_op jit(solution)/shard_map/psum | solution.py:35
  650.7 11.1 %copy-start = (f32[7168,512]{0,1:T(8,128)S(1)}, f32[7168,512]{0,1:T(8,128)}, u32[]{:S(2)}) copy-start(f32[7168,512]{0,1:T(8,128)} %all-gather.2.cloned.1.call-done) | copy-start | bytes 44040196
  660.0 1.8 copy-start.1
Sparse Core Ops, SparseCore 0:
  9.1 229.1 all-gather.1
  250.8 398.6 all-reduce.2
  670.0 395.3 all-reduce.4
where the time goes:
time: 1080 us
  waiting for transfers between devices  881 us (82%)
  blocking collectives  140 us (13%)
  matrix products  42.4 us (4%)
  between operations  13.2 us (1%)
    psum x2, waiting for transfers between devices, summer_grid(): return lax.psum(values, 'prow')  794 us
    all_to_all x1, blocking collectives, body(): lax.all_to_all(eigen_rows, 'prow', split_axis=1, concat_axis=0, tiled=True)  140 us
    all_gather x1, waiting for transfers between devices, body(): grid_vectors = lax.all_gather(reflectors, 'pcol', axis=1, tiled=True)  86 us
    dot_general x6, matrix products, matmul(): jnp.dot(left, right, precision=lax.Precision.HIGHEST, preferred_element_t...  42.4 us
  transfers between devices with their start and end apart: 3, of which 3 were waited for; matrix products, arithmetic and copies ran while one was open for 0% of the time, Pallas kernels for 0%

commit v1 on v0

--- a/solution.py
+++ b/solution.py
@@ -1,7 +1,16 @@
+import functools
 import jax
 import jax.numpy as jnp
 from jax import lax
 from jax.sharding import PartitionSpec as P
+
+
+def terms_lay(local_block, along_axis):
+    o_now = lax.all_gather(local_block, axis_name=along_axis)
+    return jnp.sum(o_now, 0)
+
+
+work_tasks = functools.partial(terms_lay, along_axis="prow")
 
 
 def upper_part(square):
@@ -32,7 +41,7 @@
     grid_vectors = lax.all_gather(reflectors, "pcol", axis=1, tiled=True)
 
     def summer_grid(values):
-        return lax.psum(values, "prow")
+        return work_tasks(values)
 
     return apply_both(grid_rows, grid_vectors, tfactors, summer_grid)
 

time: 1080 us -> 511 us (0.47)
  waiting for transfers between devices: 881 us -> 305 us
    psum x2 -> x0, waiting for transfers between devices: 794 us -> none  [summer_grid(): return lax.psum(values, 'prow')]
    all_gather x0 -> x2, waiting for transfers between devices: none -> 219 us  [terms_lay(): o_now = lax.all_gather(local_block, axis_name=along_axis)]
where the time goes in v1:
time: 511 us
  waiting for transfers between devices  305 us (60%)
  blocking collectives  140 us (27%)
  matrix products  40.6 us (8%)
  between operations  13.2 us (3%)
  local copies, waits for them, and re-layouts  7.1 us (1%)
    all_gather x2, waiting for transfers between devices, terms_lay(): o_now = lax.all_gather(local_block, axis_name=along_axis)  219 us
    all_to_all x1, blocking collectives, body(): lax.all_to_all(eigen_rows, 'prow', split_axis=1, concat_axis=0, tiled=True)  140 us
    all_gather x1, waiting for transfers between devices, body(): grid_vectors = lax.all_gather(reflectors, 'pcol', axis=1, tiled=True)  86 us
    dot_general x6, matrix products, matmul(): jnp.dot(left, right, precision=lax.Precision.HIGHEST, preferred_element_t...  40.6 us
  transfers between devices with their start and end apart: 3, of which 3 were waited for; matrix products, arithmetic and copies ran while one was open for 0% of the time, Pallas kernels for 0%

profile of v1, /device:TPU:32, one launch (start us, length us, event | category | flops | bytes accessed | tf_op | source)
XLA Modules:
  0.0 511.1 jit_solution(12965912151227493887)
XLA Ops:
  6.5 0.0 all-gather.6.cloned.1.call-start
  6.5 0.7 all-gather.6.cloned.1.call-update
  7.3 0.0 all-gather.8.cloned.1.call-start
  7.3 139.8 %all_to_all.19 = f32[4,32,7168]{2,0,1:T(4,128)} all-to-all(f32[4,32,7168]{2,0,1:T(4,128)} %bitcast.19), channel_id=1, replica_groups=mesh['prow'=32,'pcol'=8] {'prow'}, dimensions={1} | all-to-all | bytes 7340032 | tf_op jit(solution)/shard_map/all_to_all | solution.py:40
  147.1 5.3 %all_to_all.17 = f32[128,7168]{1,0:T(8,128)} reshape(f32[32,4,7168]{2,1,0:T(4,128)} %bitcast.16) | data formatting | bytes 7340032 | tf_op jit(solution)/shard_map/all_to_all | solution.py:40
  152.3 86.0 %all-gather.6.cloned.1.call-done = f32[7168,512]{0,1:T(8,128)} async-done(((f32[7168,64]{0,1:T(8,128)}), f32[7168,512]{0,1:T(8,128)}) %all-gather.6.cloned.1.call-update) | async-done | bytes 14680080 | tf_op jit(solution)/shard_map/all_gather | solution.py:41
  238.4 12.2 %fusion.4 = f32[128,256]{1,0:T(8,128)} fusion(f32[128,7168]{1,0:T(8,128)} %all_to_all.17, f32[7168,512]{0,1:T(8,128)} %all-gather.6.cloned.1.call-done), kind=kOutput, calls=%fused_computation.6 | convolution fusion | flops 2818572288 | bytes 11141120 | tf_op jit(solution)/shard_map/dot_general | solution.py:24
  250.6 0.0 copy-start.2
  250.6 0.0 all-gather.8.cloned.1.call-update
  250.6 0.2 all-gather.10.cloned.1.call-start
  250.9 112.7 %all-gather.8.cloned.1.call-done = f32[4096,256]{1,0:T(8,128)} async-done(((f32[128,256]{1,0:T(8,128)}), f32[4096,256]{1,0:T(8,128)}) %all-gather.8.cloned.1.call-update) | async-done | bytes 4194320 | tf_op jit(solution)/shard_map/all_gather | solution.py:9
  363.6 2.4 reduce_sum.18
  366.0 0.0 copy-done.2
  366.0 0.4 fusion.7
  366.4 0.0 copy-start
  366.4 9.2 %convolution_subtract_fusion.1 = f32[128,7168]{1,0:T(8,128)S(1)} fusion(f32[128,7168]{1,0:T(8,128)} %all_to_all.17, f32[128,256]{1,0:T(8,128)S(1)} %fusion.7, f32[7168,512]{0,1:T(8,128)} %all-gather.6.cloned.1.call-done), kind=kOutput, calls=%fused_computation.1 | convolution fusion | flops 2819489792 | bytes 14811136 | tf_op jit(solution)/shard_map/dot_general | solution.py:24
  375.6 0.0 copy-start.1
  375.7 1.8 copy-done.1
  377.5 0.0 copy-done
  377.5 8.0 %fusion.1 = f32[128,256]{1,0:T(8,128)} fusion(f32[128,7168]{1,0:T(8,128)S(1)} %convolution_subtract_fusion.1, f32[7168,512]{0,1:T(8,128)S(1)} %copy-done), kind=kOutput, calls=%fused_computation.3 | convolution fusion | flops 2818572288 | bytes 11141120 | tf_op jit(solution)/shard_map/dot_general | solution.py:24
  385.5 0.0 all-gather.10.cloned.1.call-update
  385.6 105.9 %all-gather.10.cloned.1.call-done = f32[4096,256]{1,0:T(8,128)} async-done(((f32[128,256]{1,0:T(8,128)}), f32[4096,256]{1,0:T(8,128)}) %all-gather.10.cloned.1.call-update) | async-done | bytes 4194320 | tf_op jit(solution)/shard_map/all_gather | solution.py:9
  491.4 2.4 reduce_sum.19
  493.9 0.4 fusion.6
  494.3 10.3 %convolution_subtract_fusion = f32[128,7168]{1,0:T(8,128)} fusion(f32[128,7168]{1,0:T(8,128)} %copy-done.1, f32[128,256]{1,0:T(8,128)S(1)} %fusion.6, f32[7168,512]{0,1:T(8,128)} %all-gather.6.cloned.1.call-done), kind=kOutput, calls=%fused_computation | convolution fusion | flops 2819489792 | bytes 14811136 | tf_op jit(solution)/shard_map/dot_general | solution.py:24
Async XLA Ops:
  6.5 231.8 %all-gather.6.cloned.1.call-start = ((), (), s32[]{:S(2)}) async-start(), calls=%async_computation.1 | async-start | bytes 16515072 | tf_op jit(solution)/shard_map/all_gather | solution.py:41
  7.3 356.3 %all-gather.8.cloned.1.call-start = ((), (), s32[]{:S(2)}) async-start(), calls=%async_computation.2 | async-start | bytes 4325376 | tf_op jit(solution)/shard_map/all_gather | solution.py:9
  250.6 115.4 %copy-start.2 = (f32[2,256,256]{2,1,0:T(8,128)S(1)}, f32[2,256,256]{2,1,0:T(8,128)}, u32[]{:S(2)}) copy-start(f32[2,256,256]{2,1,0:T(8,128)} %param.5) | copy-start | bytes 1572868
  250.6 240.8 %all-gather.10.cloned.1.call-start = ((), (), s32[]{:S(2)}) async-start(), calls=%async_computation.3 | async-start | bytes 4325376 | tf_op jit(solution)/shard_map/all_gather | solution.py:9
  366.4 11.1 %copy-start = (f32[7168,512]{0,1:T(8,128)S(1)}, f32[7168,512]{0,1:T(8,128)}, u32[]{:S(2)}) copy-start(f32[7168,512]{0,1:T(8,128)} %all-gather.6.cloned.1.call-done) | copy-start | bytes 44040196
  375.6 1.8 copy-start.1
Sparse Core Ops, SparseCore 0:
  9.1 229.1 all-gather.5
  250.8 112.7 all-gather.7
  385.7 105.6 all-gather.9
